TPU v7x, 512 devices: a whole 4x8x8 slice. The times are simulated.
512 devices in a mesh: prow: 32 (over x, z), pcol: 16 (over y, core).
Axes of the slice: x: 4, y: 8, z: 8, core: 2. Of those that a mesh axis runs over, the one named last changes fastest.
Arguments:
- matrix: float32 [8192, 12288], P('prow', 'pcol'), may hold values from -6 to 6
- pivots: int32 [512], replicated, may hold values from 128 to 8191, as said below
- lower_inverse: float32 [4, 128, 128], replicated, may hold values from -1 to 1, as said below
- upper_inverse: float32 [4, 128, 128], replicated, may hold values from -1 to 1, as said below
Outputs:
- factored: float32 [8192, 12288], P('prow', 'pcol')
Inputs may be any that keep to these rules, and one draw needn't show every extreme that they name: For a column j of panel k (k * 128 <= j < (k + 1) * 128), pivots[j] lies in [(k + 1) * 128, 8192); the 128 pivots of one panel are distinct and include (k + 1) * 128 and 8191. Each lower_inverse[k] is unit lower triangular. Each upper_inverse[k] is upper triangular with a positive diagonal.
All inputs are finite; a program needn't handle non-finite values.
Results may differ from a plain program's by a relative error of at most 0.0003.
Values sent between devices are 32-bit elements; how exact they have to be, the bound alone decides.
No kernel may reach another device: no remote copies, remote signals or barrier semaphores. Data moves between devices by JAX's collectives and lax.ppermute only.
A program may use at most 64 MiB of HBM per device.

v0:
```python
import jax
import jax.numpy as jnp
from jax import lax
from jax.sharding import PartitionSpec as P


def from_root(value, axis, source):
    kept = jnp.where(lax.axis_index(axis) == source, value, 0).astype(value.dtype)
    return lax.psum(kept, axis)


def hdot(left, right):
    return jnp.dot(left, right, precision=lax.Precision.HIGHEST, preferred_element_type=jnp.float32)


def refresh(current, pending):
    if pending is None:
        return current
    return current - hdot(pending[0], pending[1])


def per_device(matrix, pivots, lower_inverse, upper_inverse):
    rows_dev, cols_dev = matrix.shape
    width = lower_inverse.shape[1]
    prow_count = lax.axis_size("prow")
    pcol_count = lax.axis_size("pcol")
    prow_index = lax.axis_index("prow")
    pcol_index = lax.axis_index("pcol")
    local_rows = jnp.arange(rows_dev, dtype=jnp.int32)
    local_cols = jnp.arange(cols_dev, dtype=jnp.int32)
    global_rows = (local_rows // width * prow_count + prow_index) * width + local_rows % width
    global_cols = (local_cols // width * pcol_count + pcol_index) * width + local_cols % width
    current = matrix
    pending = None
    for panel_index in range(lower_inverse.shape[0]):
        first_row = panel_index * width
        past_end = first_row + width
        row_owner = panel_index % prow_count
        row_slot = panel_index // prow_count * width
        past_slot = row_slot + width
        col_owner = panel_index % pcol_count
        col_slot = panel_index // pcol_count * width
        targets = pivots[first_row:past_end]
        owner_mask = targets // width % prow_count == prow_index
        local_slots = targets // (width * prow_count) * width + targets % width
        safe_slots = jnp.where(owner_mask, local_slots, 0)
        current = refresh(current, pending)
        source = jnp.take(current, safe_slots, axis=0)
        panel_before = current[row_slot:past_slot]
        source = jnp.where(owner_mask[:, None], source, 0.0)
        at_root = prow_index == row_owner
        incoming = lax.psum(source, "prow")
        initial = from_root(panel_before, "prow", row_owner)
        current = current.at[jnp.where(owner_mask, local_slots, rows_dev)].set(initial, mode="drop")
        kept_rows = current[row_slot:past_slot]
        current = current.at[row_slot:past_slot].set(jnp.where(at_root, incoming, kept_rows))
        below_rows = global_rows >= past_end
        right_cols = global_cols >= past_end
        column = current[:, col_slot : col_slot + width]
        solved = jnp.where(below_rows[:, None], hdot(column, upper_inverse[panel_index]), 0.0)
        multipliers = from_root(solved, "pcol", col_owner)
        upper_rows = jnp.where(right_cols[None, :], hdot(lower_inverse[panel_index], incoming), 0.0)
        kept_rows = current[row_slot:past_slot]
        current = current.at[row_slot:past_slot].set(
            jnp.where(at_root & right_cols[None, :], upper_rows, kept_rows)
        )
        at_column = pcol_index == col_owner
        kept_column = current[:, col_slot : col_slot + width]
        current = current.at[:, col_slot : col_slot + width].set(
            jnp.where(at_column & below_rows[:, None], multipliers, kept_column)
        )
        pending = (multipliers, upper_rows)
    return refresh(current, pending)


def solution(mesh):
    in_specs = (P("prow", "pcol"), P(), P(), P())
    out_specs = P("prow", "pcol")
    return jax.shard_map(
        per_device, mesh=mesh, in_specs=in_specs, out_specs=out_specs, check_vma=False
    )
```

profile of v0, /device:TPU:1, one launch (start us, length us, event | category | flops | bytes accessed | tf_op | source)
XLA Modules:
  0.0 1161.3 jit_solution(9643864148377500224)
XLA Ops:
  6.5 1.1 copy.95
  7.7 0.7 copy-done.12
  8.6 0.8 gather_fusion
  9.4 0.2 copy.27
  9.5 0.8 slice-done
  10.5 1.0 select_select_fusion.3
  11.6 0.7 compare_reduce_fusion
  12.4 161.8 %all-reduce.27.cloned.1.call-done = (f32[128,768]{0,1:T(8,128)}, f32[128,768]{0,1:T(8,128)}) async-done(((f32[128,768]{0,1:T(8,128)}, f32[128,768]{0,1:T(8,128)}), (f32[128,768]{0,1:T(8,128)}, f32[128,768]{0,1:T(8,128)})) %all-reduce.27.cloned.1.call-update) | async-done | bytes 786448 | tf_op jit(solution)/shard_map/psum | solution.py:9
  174.2 1.2 copy.26
  175.3 1.4 scatter_fusion
  176.7 0.3 copy.29
  177.1 0.9 copy-done.2
  178.1 0.9 copy-done.10
  178.9 1.0 fusion.3
  180.0 0.5 fusion.7
  180.5 115.9 %all-reduce.13.cloned.1.call-done = f32[256,128]{0,1:T(8,128)} async-done(((f32[256,128]{0,1:T(8,128)}), f32[256,128]{0,1:T(8,128)}) %all-reduce.13.cloned.1.call-update) | async-done | bytes 131088 | tf_op jit(solution)/shard_map/psum | solution.py:9
  296.4 1.6 fusion.12
  298.0 0.8 convolution_subtract_fusion.3
  298.8 0.3 copy.32
  299.1 0.8 gather_fusion.1
  299.9 0.2 copy.35
  300.1 0.8 slice_select_fusion.5
  300.8 0.8 select_select_fusion.2
  301.8 158.0 %all-reduce.25.cloned.1.call-done = (f32[128,768]{0,1:T(8,128)}, f32[128,768]{0,1:T(8,128)}) async-done(((f32[128,768]{0,1:T(8,128)}, f32[128,768]{0,1:T(8,128)}), (f32[128,768]{0,1:T(8,128)}, f32[128,768]{0,1:T(8,128)})) %all-reduce.25.cloned.1.call-update) | async-done | bytes 786448 | tf_op jit(solution)/shard_map/psum | solution.py:9
  459.8 1.2 copy.33
  461.0 1.4 scatter_fusion.1
  462.4 0.3 copy.37
  462.7 0.9 copy-done.3
  463.7 1.0 fusion.2
  464.8 0.5 fusion.6
  465.3 115.9 %all-reduce.15.cloned.1.call-done = f32[256,128]{0,1:T(8,128)} async-done(((f32[256,128]{0,1:T(8,128)}), f32[256,128]{0,1:T(8,128)}) %all-reduce.15.cloned.1.call-update) | async-done | bytes 131088 | tf_op jit(solution)/shard_map/psum | solution.py:9
  581.1 1.6 fusion.13
  582.8 0.8 convolution_subtract_fusion.2
  583.6 0.3 copy.40
  583.8 0.8 gather_fusion.2
  584.7 0.2 copy.43
  584.8 0.8 slice_select_fusion.3
  585.6 0.8 select_select_fusion.1
  586.6 158.0 %all-reduce.23.cloned.1.call-done = (f32[128,768]{0,1:T(8,128)}, f32[128,768]{0,1:T(8,128)}) async-done(((f32[128,768]{0,1:T(8,128)}, f32[128,768]{0,1:T(8,128)}), (f32[128,768]{0,1:T(8,128)}, f32[128,768]{0,1:T(8,128)})) %all-reduce.23.cloned.1.call-update) | async-done | bytes 786448 | tf_op jit(solution)/shard_map/psum | solution.py:9
  744.6 1.2 copy.41
  745.8 1.4 scatter_fusion.2
  747.2 0.3 copy.45
  747.5 0.9 copy-done.4
  748.5 1.0 fusion.1
  749.6 0.5 fusion.5
  750.1 115.9 %all-reduce.17.cloned.1.call-done = f32[256,128]{0,1:T(8,128)} async-done(((f32[256,128]{0,1:T(8,128)}), f32[256,128]{0,1:T(8,128)}) %all-reduce.17.cloned.1.call-update) | async-done | bytes 131088 | tf_op jit(solution)/shard_map/psum | solution.py:9
  865.9 1.7 fusion.14
  867.6 0.8 convolution_subtract_fusion.1
  868.4 0.3 copy.48
  868.7 0.8 gather_fusion.3
  869.5 0.2 copy.51
  869.6 0.8 slice_select_fusion.1
  870.4 0.8 select_select_fusion
  871.4 158.0 %all-reduce.21.cloned.1.call-done = (f32[128,768]{0,1:T(8,128)}, f32[128,768]{0,1:T(8,128)}) async-done(((f32[128,768]{0,1:T(8,128)}, f32[128,768]{0,1:T(8,128)}), (f32[128,768]{0,1:T(8,128)}, f32[128,768]{0,1:T(8,128)})) %all-reduce.21.cloned.1.call-update) | async-done | bytes 786448 | tf_op jit(solution)/shard_map/psum | solution.py:9
  1029.4 1.2 copy.49
  1030.5 1.6 scatter_fusion.3
  1032.1 0.3 copy.53
  1032.4 0.9 copy-done.5
  1033.4 1.0 fusion
  1034.4 0.5 fusion.4
  1034.9 115.9 %all-reduce.19.cloned.1.call-done = f32[256,128]{0,1:T(8,128)} async-done(((f32[256,128]{0,1:T(8,128)}), f32[256,128]{0,1:T(8,128)}) %all-reduce.19.cloned.1.call-update) | async-done | bytes 131088 | tf_op jit(solution)/shard_map/psum | solution.py:9
  1150.9 1.7 fusion.15
  1152.5 0.8 convolution_subtract_fusion
  1153.3 1.1 copy.56
  (70 shorter events, 1.5 us)
Async XLA Ops:
  6.5 167.6 %all-reduce.27.cloned.1.call-start = ((), (), s32[]{:S(2)}) async-start(), calls=%async_computation.7 | async-start | bytes 1572864 | tf_op jit(solution)/shard_map/psum | solution.py:9
  7.7 0.9 copy-start
  7.7 0.7 copy-start.12
  9.4 1.0 slice-start
  11.5 163.8 %copy-start.1 = (f32[256,768]{1,0:T(8,128)S(1)}, f32[256,768]{1,0:T(8,128)}, u32[]{:S(2)}) copy-start(f32[256,768]{1,0:T(8,128)} %copy-done) | copy-start | bytes 2359300
  11.5 284.8 %all-reduce.13.cloned.1.call-start = ((), (), s32[]{:S(2)}) async-start(), calls=%async_computation | async-start | bytes 262144 | tf_op jit(solution)/shard_map/psum | solution.py:9
  177.0 1.0 copy-start.2
  178.0 0.9 copy-start.10
  178.9 1.1 copy-start.11
  179.9 279.9 %all-reduce.25.cloned.1.call-start = ((), (), s32[]{:S(2)}) async-start(), calls=%async_computation.6 | async-start | bytes 1572864 | tf_op jit(solution)/shard_map/psum | solution.py:9
  296.4 1.7 copy-start.6
  301.7 279.5 %all-reduce.15.cloned.1.call-start = ((), (), s32[]{:S(2)}) async-start(), calls=%async_computation.1 | async-start | bytes 262144 | tf_op jit(solution)/shard_map/psum | solution.py:9
  462.6 1.0 copy-start.3
  464.7 279.9 %all-reduce.23.cloned.1.call-start = ((), (), s32[]{:S(2)}) async-start(), calls=%async_computation.5 | async-start | bytes 1572864 | tf_op jit(solution)/shard_map/psum | solution.py:9
  581.1 1.7 copy-start.7
  586.4 279.5 %all-reduce.17.cloned.1.call-start = ((), (), s32[]{:S(2)}) async-start(), calls=%async_computation.2 | async-start | bytes 262144 | tf_op jit(solution)/shard_map/psum | solution.py:9
  747.4 1.0 copy-start.4
  749.5 279.9 %all-reduce.21.cloned.1.call-start = ((), (), s32[]{:S(2)}) async-start(), calls=%async_computation.4 | async-start | bytes 1572864 | tf_op jit(solution)/shard_map/psum | solution.py:9
  865.9 1.7 copy-start.8
  871.2 279.6 %all-reduce.19.cloned.1.call-start = ((), (), s32[]{:S(2)}) async-start(), calls=%async_computation.3 | async-start | bytes 262144 | tf_op jit(solution)/shard_map/psum | solution.py:9
  1032.4 1.0 copy-start.5
  1150.9 1.7 copy-start.9
Sparse Core Ops, SparseCore 0:
  11.7 162.4 all-reduce.26
  180.1 116.2 all-reduce.12
  301.8 157.9 all-reduce.24
  464.8 116.2 all-reduce.14
  586.5 158.0 all-reduce.22
  749.6 116.2 all-reduce.16
  871.4 157.9 all-reduce.20
  1034.6 116.2 all-reduce.18
where the time goes:
time: 1160 us
  waiting for transfers between devices  1100 us (95%)
  local copies, waits for them, and re-layouts  24.9 us (2%)
  between operations  14 us (1%)
  other arithmetic  13.6 us (1%)
    psum x8, waiting for transfers between devices, from_root(): return lax.psum(kept, axis)  1100 us
  transfers between devices with their start and end apart: 8, of which 8 were waited for; matrix products, arithmetic and copies ran while one was open for 0% of the time, Pallas kernels for 0%

commit v1 on v0

--- a/solution.py
+++ b/solution.py
@@ -6,7 +6,7 @@
 
 def from_root(value, axis, source):
     kept = jnp.where(lax.axis_index(axis) == source, value, 0).astype(value.dtype)
-    return lax.psum(kept, axis)
+    return jnp.sum(lax.all_gather(kept, axis), axis=0)
 
 
 def hdot(left, right):

time: 1160 us -> 1370 us (1.18)
  waiting for transfers between devices: 1100 us -> 1220 us
  local copies, waits for them, and re-layouts: 24.9 us -> 62.8 us
  other arithmetic: 13.6 us -> 46 us
    all_gather x0 -> x8, waiting for transfers between devices: none -> 676 us  [from_root(): return jnp.sum(lax.all_gather(kept, axis), axis=0)]
    psum x8 -> x4, waiting for transfers between devices: 1100 us -> 547 us  [per_device(): incoming = lax.psum(source, 'prow')]
    unnamed x32 -> x14, local copies, waits for them, and re-layouts: 6.93 us -> 49.3 us
    reduce_sum x0 -> x8, other arithmetic: none -> 34 us  [from_root(): return jnp.sum(lax.all_gather(kept, axis), axis=0)]
  transfers between devices with their start and end apart: 8 -> 12, of which waited for: 8 -> 12; matrix products, arithmetic and copies ran while one was open for 0% -> 7% of each run, Pallas kernels for 0% -> 0%
where the time goes in v1:
time: 1370 us; the launch traced here: 1360 us
  waiting for transfers between devices  1220 us (89%)
  local copies, waits for them, and re-layouts  62.8 us (5%)
  other arithmetic  46 us (3%)
  between operations  14.3 us (1%)
  matrix products  13.8 us (1%)
    all_gather x8, waiting for transfers between devices, from_root(): return jnp.sum(lax.all_gather(kept, axis), axis=0)  676 us
    psum x4, waiting for transfers between devices, per_device(): incoming = lax.psum(source, 'prow')  547 us
    unnamed x14, local copies, waits for them, and re-layouts  49.3 us
    reduce_sum x8, other arithmetic, from_root(): return jnp.sum(lax.all_gather(kept, axis), axis=0)  34 us
  transfers between devices with their start and end apart: 12, of which 12 were waited for; matrix products, arithmetic and copies ran while one was open for 7% of the time, Pallas kernels for 0%

profile of v1, /device:TPU:1, one launch (start us, length us, event | category | flops | bytes accessed | tf_op | source)
XLA Modules:
  0.0 1361.6 jit_solution(17678542416162495034)
XLA Ops:
  6.5 1.1 copy.106
  7.9 0.8 broadcast_select_fusion
  8.7 0.9 compare_and_fusion
  9.6 0.8 gather_fusion
  10.6 0.8 select_select_fusion.3
  11.5 132.7 %all-gather.17.cloned.1.call-done = f32[4096,768]{0,1:T(8,128)} async-done(((f32[128,768]{0,1:T(8,128)}), f32[4096,768]{0,1:T(8,128)}) %all-gather.17.cloned.1.call-update) | async-done | bytes 12582928 | tf_op jit(solution)/shard_map/all_gather | solution.py:9
  144.2 12.0 copy.81
  156.1 6.8 bitcast_reduce_fusion.3
  163.2 1.4 scatter_fusion
  164.5 0.3 copy.48
  164.9 136.8 %all-reduce.5.cloned.1.call-done = f32[128,768]{0,1:T(8,128)} async-done(((f32[128,768]{0,1:T(8,128)}), f32[128,768]{0,1:T(8,128)}) %all-reduce.5.cloned.1.call-update) | async-done | bytes 393232 | tf_op jit(solution)/shard_map/psum | solution.py:52
  301.6 1.1 fusion.8
  302.7 1.0 fusion.3
  303.9 0.7 compare_reduce_fusion
  304.6 1.6 fusion.7
  306.2 41.3 %all-gather.19.cloned.1.call-done = f32[4096,128]{1,0:T(8,128)} async-done(((f32[256,128]{1,0:T(8,128)}), f32[4096,128]{1,0:T(8,128)}) %all-gather.19.cloned.1.call-update) | async-done | bytes 2097168 | tf_op jit(solution)/shard_map/all_gather | solution.py:9
  347.5 1.7 reduce_sum.73
  349.3 0.6 fusion.12
  349.9 0.8 convolution_subtract_fusion.3
  350.7 0.8 slice_select_fusion.5
  351.9 0.8 gather_fusion.1
  352.9 0.8 select_select_fusion.2
  353.7 0.5 all-gather.23.cloned.1.call-start
  354.2 124.3 %all-gather.21.cloned.1.call-done = f32[4096,768]{0,1:T(8,128)} async-done(((f32[128,768]{0,1:T(8,128)}), f32[4096,768]{0,1:T(8,128)}) %all-gather.21.cloned.1.call-update) | async-done | bytes 12582928 | tf_op jit(solution)/shard_map/all_gather | solution.py:9
  478.6 12.0 copy.82
  490.5 6.8 bitcast_reduce_fusion.2
  497.5 1.4 scatter_fusion.1
  498.9 0.3 copy.56
  499.2 136.6 %all-reduce.7.cloned.1.call-done = f32[128,768]{0,1:T(8,128)} async-done(((f32[128,768]{0,1:T(8,128)}), f32[128,768]{0,1:T(8,128)}) %all-reduce.7.cloned.1.call-update) | async-done | bytes 393232 | tf_op jit(solution)/shard_map/psum | solution.py:52
  635.9 1.0 fusion.2
  637.1 1.6 fusion.6
  638.7 42.8 %all-gather.23.cloned.1.call-done = f32[4096,128]{1,0:T(8,128)} async-done(((f32[256,128]{1,0:T(8,128)}), f32[4096,128]{1,0:T(8,128)}) %all-gather.23.cloned.1.call-update) | async-done | bytes 2097168 | tf_op jit(solution)/shard_map/all_gather | solution.py:9
  681.5 1.7 reduce_sum.75
  683.3 0.6 fusion.13
  683.9 0.8 convolution_subtract_fusion.2
  684.7 0.8 slice_select_fusion.3
  685.9 0.8 gather_fusion.2
  686.9 0.8 select_select_fusion.1
  688.0 124.6 %all-gather.25.cloned.1.call-done = f32[4096,768]{0,1:T(8,128)} async-done(((f32[128,768]{0,1:T(8,128)}), f32[4096,768]{0,1:T(8,128)}) %all-gather.25.cloned.1.call-update) | async-done | bytes 12582928 | tf_op jit(solution)/shard_map/all_gather | solution.py:9
  812.6 12.0 copy.83
  824.5 6.8 bitcast_reduce_fusion.1
  831.5 1.4 scatter_fusion.2
  833.2 136.8 %all-reduce.9.cloned.1.call-done = f32[128,768]{0,1:T(8,128)} async-done(((f32[128,768]{0,1:T(8,128)}), f32[128,768]{0,1:T(8,128)}) %all-reduce.9.cloned.1.call-update) | async-done | bytes 393232 | tf_op jit(solution)/shard_map/psum | solution.py:52
  970.1 1.0 fusion.1
  971.3 1.6 fusion.5
  972.9 43.0 %all-gather.27.cloned.1.call-done = f32[4096,128]{1,0:T(8,128)} async-done(((f32[256,128]{1,0:T(8,128)}), f32[4096,128]{1,0:T(8,128)}) %all-gather.27.cloned.1.call-update) | async-done | bytes 2097168 | tf_op jit(solution)/shard_map/all_gather | solution.py:9
  1015.9 1.7 reduce_sum.77
  1017.7 0.6 fusion.14
  1018.3 0.8 convolution_subtract_fusion.1
  1019.1 0.8 slice_select_fusion.1
  1020.3 0.8 gather_fusion.3
  1021.3 0.8 select_select_fusion
  1022.4 124.6 %all-gather.29.cloned.1.call-done = f32[4096,768]{0,1:T(8,128)} async-done(((f32[128,768]{0,1:T(8,128)}), f32[4096,768]{0,1:T(8,128)}) %all-gather.29.cloned.1.call-update) | async-done | bytes 12582928 | tf_op jit(solution)/shard_map/all_gather | solution.py:9
  1147.0 12.0 copy.84
  1158.9 6.8 bitcast_reduce_fusion
  1165.9 1.4 scatter_fusion.3
  1167.6 136.8 %all-reduce.11.cloned.1.call-done = f32[128,768]{0,1:T(8,128)} async-done(((f32[128,768]{0,1:T(8,128)}), f32[128,768]{0,1:T(8,128)}) %all-reduce.11.cloned.1.call-update) | async-done | bytes 393232 | tf_op jit(solution)/shard_map/psum | solution.py:52
  1304.5 1.0 fusion
  1305.6 1.6 fusion.4
  1307.2 42.9 %all-gather.31.cloned.1.call-done = f32[4096,128]{1,0:T(8,128)} async-done(((f32[256,128]{1,0:T(8,128)}), f32[4096,128]{1,0:T(8,128)}) %all-gather.31.cloned.1.call-update) | async-done | bytes 2097168 | tf_op jit(solution)/shard_map/all_gather | solution.py:9
  1350.1 1.7 reduce_sum.79
  1351.9 0.6 fusion.15
  1352.6 0.8 convolution_subtract_fusion
  1353.3 1.1 copy.75
  (77 shorter events, 4.8 us)
Async XLA Ops:
  6.5 137.6 %all-gather.17.cloned.1.call-start = ((), (), s32[]{:S(2)}) async-start(), calls=%async_computation.4 | async-start | bytes 12976128 | tf_op jit(solution)/shard_map/all_gather | solution.py:9
  8.7 293.0 %all-reduce.5.cloned.1.call-start = ((), (), s32[]{:S(2)}) async-start(), calls=%async_computation | async-start | bytes 786432 | tf_op jit(solution)/shard_map/psum | solution.py:52
  11.4 336.0 %all-gather.19.cloned.1.call-start = ((), (), s32[]{:S(2)}) async-start(), calls=%async_computation.5 | async-start | bytes 2228224 | tf_op jit(solution)/shard_map/all_gather | solution.py:9
  156.1 146.6 %copy-start = (f32[4,128,128]{2,1,0:T(8,128)S(1)}, f32[4,128,128]{2,1,0:T(8,128)}, u32[]{:S(2)}) copy-start(f32[4,128,128]{2,1,0:T(8,128)} %param.33) | copy-start | bytes 786436
  156.1 148.4 %copy-start.1 = (f32[4,128,128]{2,1,0:T(8,128)S(1)}, f32[4,128,128]{2,1,0:T(8,128)}, u32[]{:S(2)}) copy-start(f32[4,128,128]{2,1,0:T(8,128)} %param.32) | copy-start | bytes 786436
  303.8 174.8 %all-gather.21.cloned.1.call-start = ((), (), s32[]{:S(2)}) async-start(), calls=%async_computation.6 | async-start | bytes 12976128 | tf_op jit(solution)/shard_map/all_gather | solution.py:9
  351.5 284.3 %all-reduce.7.cloned.1.call-start = ((), (), s32[]{:S(2)}) async-start(), calls=%async_computation.1 | async-start | bytes 786432 | tf_op jit(solution)/shard_map/psum | solution.py:52
  353.7 327.8 %all-gather.23.cloned.1.call-start = ((), (), s32[]{:S(2)}) async-start(), calls=%async_computation.7 | async-start | bytes 2228224 | tf_op jit(solution)/shard_map/all_gather | solution.py:9
  637.0 175.6 %all-gather.25.cloned.1.call-start = ((), (), s32[]{:S(2)}) async-start(), calls=%async_computation.8 | async-start | bytes 12976128 | tf_op jit(solution)/shard_map/all_gather | solution.py:9
  685.5 284.5 %all-reduce.9.cloned.1.call-start = ((), (), s32[]{:S(2)}) async-start(), calls=%async_computation.2 | async-start | bytes 786432 | tf_op jit(solution)/shard_map/psum | solution.py:52
  687.7 328.1 %all-gather.27.cloned.1.call-start = ((), (), s32[]{:S(2)}) async-start(), calls=%async_computation.9 | async-start | bytes 2228224 | tf_op jit(solution)/shard_map/all_gather | solution.py:9
  971.2 175.8 %all-gather.29.cloned.1.call-start = ((), (), s32[]{:S(2)}) async-start(), calls=%async_computation.10 | async-start | bytes 12976128 | tf_op jit(solution)/shard_map/all_gather | solution.py:9
  1019.9 284.5 %all-reduce.11.cloned.1.call-start = ((), (), s32[]{:S(2)}) async-start(), calls=%async_computation.3 | async-start | bytes 786432 | tf_op jit(solution)/shard_map/psum | solution.py:52
  1022.1 328.0 %all-gather.31.cloned.1.call-start = ((), (), s32[]{:S(2)}) async-start(), calls=%async_computation.11 | async-start | bytes 2228224 | tf_op jit(solution)/shard_map/all_gather | solution.py:9
Sparse Core Ops, SparseCore 0:
  10.4 133.7 all-gather.16
  147.6 154.0 all-reduce.4
  303.9 43.5 all-gather.18
  351.6 126.8 all-gather.20
  481.8 153.9 all-reduce.6
  637.8 43.6 all-gather.22
  685.7 126.8 all-gather.24
  816.0 154.0 all-reduce.8
  972.2 43.6 all-gather.26
  1020.0 126.8 all-gather.28
  1150.4 154.0 all-reduce.10
  1306.4 43.6 all-gather.30
